TPU v7x, 32 devices: a whole 2x2x4 slice. The times are simulated.
32 devices in a mesh: grp: 2 (over core), dev: 16 (over z, y, x).
Axes of the slice: x: 2, y: 2, z: 4, core: 2. Of those that a mesh axis runs over, the one named last changes fastest.
Arguments:
- queries: float32 [32, 12, 128], P(('grp', 'dev')), may hold values from -2.1 to 2.1
- pages: float32 [32, 256, 128], P(('grp', 'dev')), may hold values from -2.1 to 2.1
- positive: int32 [32], replicated, may hold values from 0 to 31
Outputs:
- loss: float32 [], replicated
- question_token_slope: float32 [32, 12, 128], P(('grp', 'dev'))
- page_grad: float32 [32, 256, 128], P(('grp', 'dev'))
All inputs are finite; a program needn't handle non-finite values.
Results may differ from a plain program's by a relative error of at most 0.00019.
Values sent between devices are 32-bit elements; how exact they have to be, the bound alone decides.
A program may use at most 64 MiB of HBM per device.

v0:
```python
import jax
import jax.numpy as jnp
from jax import lax
from jax.sharding import PartitionSpec as P

cap_value = 4.0
sharpness_divisor = 0.25
logit_scale = 8.0
z_weight = 0.001
highest = lax.Precision.HIGHEST


def block_partial_terms(query_rows, page_rows, query_tokens):
    scores = jnp.dot(query_rows, page_rows.T, precision=highest, preferred_element_type=jnp.float32)
    tangent = jnp.tanh(scores / cap_value)
    bounded_similarity = cap_value * tangent
    exponential_grid = jnp.exp(bounded_similarity / sharpness_divisor)
    accumulated_totals = jnp.sum(exponential_grid, axis=1)
    gentle_peak = sharpness_divisor * jnp.log(accumulated_totals)
    slopes = (
        exponential_grid
        / accumulated_totals[:, None]
        * (1.0 - tangent * tangent)
        * (logit_scale / query_tokens)
    )
    return (gentle_peak, slopes)


def shards(queries, pages, positive):
    gathered = lax.all_gather(queries, ("grp", "dev"), axis=0, tiled=True)
    query_count, query_tokens, feature_width = gathered.shape
    page_rows = pages[0]
    page_index = lax.axis_index(("grp", "dev"))
    block_size = 16
    block_count = query_count // block_size
    query_blocks = gathered.reshape(block_count, block_size * query_tokens, feature_width)
    chosen = (positive == page_index).astype(jnp.float32)

    def block_logits(gentle_peak):
        return (
            logit_scale / query_tokens * gentle_peak.reshape(block_size, query_tokens).sum(axis=1)
        )

    def evaluate_loss_and_slopes(query_rows):
        gentle_peak, slopes = block_partial_terms(query_rows, page_rows, query_tokens)
        unscaled = jnp.dot(slopes, page_rows, precision=highest, preferred_element_type=jnp.float32)
        return (block_logits(gentle_peak), unscaled)

    logits, unscaled = lax.map(evaluate_loss_and_slopes, query_blocks)
    statistics_logits = logits.reshape(query_count)
    exponential_grid = jnp.exp(statistics_logits)
    accumulated_totals, matching_logit = lax.psum(
        (exponential_grid, chosen * statistics_logits), ("grp", "dev")
    )
    log_totals = jnp.log(accumulated_totals)
    loss = jnp.mean(log_totals - matching_logit + z_weight * log_totals * log_totals)
    coefficients = (
        (1.0 + 2.0 * z_weight * log_totals) * exponential_grid / accumulated_totals - chosen
    ) / query_count
    loss, coefficients = (loss, coefficients)
    factors = jnp.repeat(coefficients, query_tokens).reshape(
        block_count, block_size * query_tokens, 1
    )
    query_terms = unscaled * factors

    def page_only(page_total, inputs):
        query_rows, factor_rows = inputs
        unused_smooth, slopes = block_partial_terms(query_rows, page_rows, query_tokens)
        token_grads = slopes * factor_rows
        page_total = page_total + jnp.dot(
            token_grads.T, query_rows, precision=highest, preferred_element_type=jnp.float32
        )
        return (page_total, None)

    page_start = jnp.zeros(page_rows.shape, jnp.float32)
    page_total, unused_outputs = lax.scan(page_only, page_start, (query_blocks, factors))
    query_terms = query_terms.reshape(query_count, query_tokens, feature_width)
    summed = lax.psum(query_terms, ("grp", "dev"))
    own_count = queries.shape[0]
    question_token_slope = lax.dynamic_slice_in_dim(summed, page_index * own_count, own_count, 0)
    return (loss, question_token_slope, page_total[None])


def solution(mesh):
    return jax.shard_map(
        shards,
        mesh=mesh,
        in_specs=(P(("grp", "dev"), None, None), P(("grp", "dev"), None, None), P()),
        out_specs=(P(), P(("grp", "dev"), None, None), P(("grp", "dev"), None, None)),
        check_vma=False,
    )
```

profile of v0, /device:TPU:0, one launch (start us, length us, event | category | flops | bytes accessed | tf_op | source)
XLA Modules:
  0.0 258.3 jit_solution(4730078051259543547)
XLA Ops:
  7.2 0.7 copy-done.1
  7.9 71.4 %all_gather.3 = f32[32,12,128]{2,1,0:T(8,128)S(1)} all-gather(f32[1,12,128]{2,1,0:T(8,128)S(1)} %copy.13), channel_id=1, replica_groups=mesh['grp'=2,'dev'=16] {'grp','dev'}, dimensions={0}, use_global_device_ids=true | all-gather | bytes 202752 | tf_op jit(solution)/shard_map/all_gather | solution.py:30
  79.3 0.9 copy-done
  80.2 2.2 while.27
  80.2 0.4 fusion.57
  80.7 0.4 fusion.58
  81.2 0.1 reduce_sum.54
  81.3 0.4 fusion.57
  81.8 0.4 fusion.58
  82.3 0.1 reduce_sum.54
  82.5 0.7 copy-done.2
  83.2 36.8 %all-reduce = (f32[32]{0:T(128)S(1)}, f32[32]{0:T(128)S(1)}) all-reduce(f32[32]{0:T(128)S(1)} %get-tuple-element.208, f32[32]{0:T(128)S(1)} %get-tuple-element.207), channel_id=1, replica_groups=mesh['grp'=2,'dev'=16] {'grp','dev'}, use_global_device_ids=true, to_apply=%region_5.6 | all-reduce | flops 64 | bytes 512 | tf_op jit(solution)/shard_map/psum | solution.py:52
  120.0 0.6 fusion.39
  120.7 0.1 broadcast_in_dim.36
  120.8 0.1 broadcast_multiply_fusion
  121.0 0.7 reshape.47
  121.8 2.5 while.28
  121.8 0.4 fusion.62
  122.3 0.8 convolution_add_fusion.2
  123.1 0.4 fusion.62
  123.5 0.8 convolution_add_fusion.2
  125.0 124.0 %all-reduce.3.cloned.1.call-done = f32[32,12,128]{2,1,0:T(8,128)} async-done(((f32[32,12,128]{2,1,0:T(8,128)}), f32[32,12,128]{2,1,0:T(8,128)}) %all-reduce.3.cloned.1.call-update) | async-done | bytes 196624 | tf_op jit(solution)/shard_map/psum | solution.py:78
  249.0 0.7 constant_dynamic-slice_fusion
  249.7 0.6 copy.15
  (27 shorter events, 0.7 us)
Async XLA Ops:
  7.2 241.8 %all-reduce.3.cloned.1.call-start = ((), (), s32[]{:S(2)}) async-start(), calls=%async_computation | async-start | bytes 524288 | tf_op jit(solution)/shard_map/psum | solution.py:78
  7.2 0.7 copy-start.1
  79.3 0.9 copy-start
  82.5 0.7 copy-start.2
  124.3 126.0 %copy-start.3 = (f32[256,128]{1,0:T(8,128)}, f32[256,128]{1,0:T(8,128)S(1)}, u32[]{:S(2)}) copy-start(f32[256,128]{1,0:T(8,128)S(1)} %get-tuple-element.136) | copy-start | bytes 393220
Sparse Core Ops, SparseCore 0:
  121.8 127.1 all-reduce.2
where the time goes:
time: 259 us; the launch traced here: 258 us
  waiting for transfers between devices  124 us (48%)
  blocking collectives  108 us (42%)
  between operations  15.9 us (6%)
  local copies, waits for them, and re-layouts  4.91 us (2%)
  matrix products  4.08 us (2%)
    psum x1, waiting for transfers between devices, shards(): summed = lax.psum(query_terms, ('grp', 'dev'))  124 us
    all_gather x1, blocking collectives, shards(): gathered = lax.all_gather(queries, ('grp', 'dev'), axis=0, tiled=True)  71.4 us
    psum x1, blocking collectives, shards(): lax.psum((exponential_grid, chosen * statistics_logits), ('grp', 'dev'))  36.8 us
  transfers between devices with their start and end apart: 1, of which 1 were waited for; matrix products, arithmetic and copies ran while one was open for 1% of the time, Pallas kernels for 0%

commit v1 on v0

--- a/solution.py
+++ b/solution.py
@@ -1,3 +1,4 @@
+import functools
 import jax
 import jax.numpy as jnp
 from jax import lax
@@ -8,6 +9,14 @@
 logit_scale = 8.0
 z_weight = 0.001
 highest = lax.Precision.HIGHEST
+
+
+def _expand_row(local_x, axis_id):
+    reply = jnp.sum(lax.all_gather(local_x, axis_id), 0)
+    return reply
+
+
+_set_object = functools.partial(_expand_row, axis_id=("grp", "dev"))
 
 
 def block_partial_terms(query_rows, page_rows, query_tokens):
@@ -75,7 +84,7 @@
     page_start = jnp.zeros(page_rows.shape, jnp.float32)
     page_total, unused_outputs = lax.scan(page_only, page_start, (query_blocks, factors))
     query_terms = query_terms.reshape(query_count, query_tokens, feature_width)
-    summed = lax.psum(query_terms, ("grp", "dev"))
+    summed = _set_object(query_terms)
     own_count = queries.shape[0]
     question_token_slope = lax.dynamic_slice_in_dim(summed, page_index * own_count, own_count, 0)
     return (loss, question_token_slope, page_total[None])

time: 259 us -> 206 us (0.80)
  waiting for transfers between devices: 124 us -> 64.7 us
  matrix products: 4.08 us -> 9.5 us
  other arithmetic: 1.01 us -> 4.41 us
    psum x1 -> x0, waiting for transfers between devices: 124 us -> none  [shards(): summed = lax.psum(query_terms, ('grp', 'dev'))]
    all_gather x0 -> x1, waiting for transfers between devices: none -> 64.7 us  [_expand_row(): reply = jnp.sum(lax.all_gather(local_x, axis_id), 0)]
    dot_general x4, matrix products: 1.79 us -> 5.41 us  [block_partial_terms(): jnp.dot(query_rows, page_rows.T, precision=highest, preferred_element_typ...]
    reduce_sum x0 -> x1, other arithmetic: none -> 3.4 us  [_expand_row(): reply = jnp.sum(lax.all_gather(local_x, axis_id), 0)]
  transfers between devices with their start and end apart: 1 -> 1, of which waited for: 1 -> 1; matrix products, arithmetic and copies ran while one was open for 1% -> 2% of each run, Pallas kernels for 0% -> 0%
where the time goes in v1:
time: 206 us
  blocking collectives  108 us (52%)
  waiting for transfers between devices  64.7 us (31%)
  between operations  15.9 us (8%)
  matrix products  9.5 us (5%)
  other arithmetic  4.41 us (2%)
  local copies, waits for them, and re-layouts  2.74 us (1%)
    all_gather x1, blocking collectives, shards(): gathered = lax.all_gather(queries, ('grp', 'dev'), axis=0, tiled=True)  71.4 us
    all_gather x1, waiting for transfers between devices, _expand_row(): reply = jnp.sum(lax.all_gather(local_x, axis_id), 0)  64.7 us
    psum x1, blocking collectives, shards(): lax.psum((exponential_grid, chosen * statistics_logits), ('grp', 'dev'))  36.8 us
    dot_general x4, matrix products, block_partial_terms(): jnp.dot(query_rows, page_rows.T, precision=highest, preferred_element_typ...  5.41 us
  transfers between devices with their start and end apart: 1, of which 1 were waited for; matrix products, arithmetic and copies ran while one was open for 2% of the time, Pallas kernels for 0%

profile of v1, /device:TPU:0, one launch (start us, length us, event | category | flops | bytes accessed | tf_op | source)
XLA Modules:
  0.0 205.7 jit_solution(10949903801709902702)
XLA Ops:
  7.2 0.7 copy.14
  7.9 71.4 %all_gather.6 = f32[32,12,128]{2,1,0:T(8,128)S(1)} all-gather(f32[1,12,128]{2,1,0:T(8,128)S(1)} %copy.14), channel_id=1, replica_groups=mesh['grp'=2,'dev'=16] {'grp','dev'}, dimensions={0}, use_global_device_ids=true | all-gather | bytes 202752 | tf_op jit(solution)/shard_map/all_gather | solution.py:39
  79.4 5.8 %while.27 = (s32[]{:T(128)}, f32[2,16]{1,0:T(2,128)S(1)}, f32[2,192,128]{2,1,0:T(8,128)S(1)}, f32[2,192,128]{2,1,0:T(8,128)S(1)}, f32[256,128]{1,0:T(8,128)}, /*index=5*/s32[]{:T(128)}, f32[]{:T(128)}, s32[]{:T(128)}) while((s32[]{:T(128)}, f32[2,16]{1,0:T(2,128)S(1)}, f32[2,192,128]{2,1,0:T(8,128)S(1)}, f32[2,192,128]{2,1,0:T(8,128)S(1)}, ...), condition=%wide.region_3.4_spmd, body=%wide.region_0.3_spmd.sunk | while | flops 151437504 | bytes 858029 | solution.py:58
  79.4 1.4 fusion.57
  80.7 1.3 fusion.58
  82.1 0.1 reduce_sum.64
  82.3 1.4 fusion.57
  83.6 1.3 fusion.58
  85.0 0.1 reduce_sum.64
  85.2 0.1 reshape.43
  85.3 36.8 %all-reduce = (f32[32]{0:T(128)S(1)}, f32[32]{0:T(128)S(1)}) all-reduce(f32[32]{0:T(128)S(1)} %get-tuple-element.205, f32[32]{0:T(128)S(1)} %get-tuple-element.204), channel_id=1, replica_groups=mesh['grp'=2,'dev'=16] {'grp','dev'}, use_global_device_ids=true, to_apply=%region_5.6 | all-reduce | flops 64 | bytes 512 | tf_op jit(solution)/shard_map/psum | solution.py:61
  122.1 0.6 fusion.39
  122.9 0.1 broadcast_in_dim.36
  123.0 0.1 broadcast_multiply_fusion
  123.1 0.7 copy.15
  123.9 0.1 broadcast_in_dim.40
  124.7 4.3 %while.28 = (s32[]{:T(128)}, f32[256,128]{1,0:T(8,128)S(1)}, f32[2,192,128]{2,1,0:T(8,128)S(1)}, f32[256,128]{1,0:T(8,128)}, f32[2,192,1]{1,2,0:T(1,128)S(1)}, /*index=5*/s32[]{:T(128)}, s32[]{:T(128)}) while((s32[]{:T(128)}, f32[256,128]{1,0:T(8,128)S(1)}, f32[2,192,128]{2,1,0:T(8,128)S(1)}, f32[256,128]{1,0:T(8,128)}, ...), condition=%wide.region_10.11_spmd.clone, body=%wide.region_8.10_spmd.clone.sunk | while | flops 151502848 | bytes 987499 | solution.py:85
  124.7 1.4 fusion.62
  126.0 0.8 convolution_add_fusion.2
  126.9 1.4 fusion.62
  128.2 0.8 convolution_add_fusion.2
  129.0 64.7 %all-gather.2.cloned.1.call-done = f32[32,32,12,128]{3,1,2,0:T(8,128)} async-done(((f32[1,32,12,128]{3,1,2,0:T(8,128)}), f32[32,32,12,128]{3,1,2,0:T(8,128)}) %all-gather.2.cloned.1.call-update) | async-done | bytes 6291472 | tf_op jit(solution)/shard_map/all_gather | solution.py:15
  193.7 3.4 %reduce_sum.55 = f32[32,12,128]{2,0,1:T(8,128)S(1)} reduce(f32[32,32,12,128]{3,1,2,0:T(8,128)} %all-gather.2.cloned.1.call-done, f32[]{:T(128)} %constant.120.clone.1), dimensions={0}, to_apply=%region_7.8 | reduce | flops 1523712 | bytes 6488068 | tf_op jit(solution)/shard_map/reduce_sum | solution.py:15
  197.1 0.6 constant_dynamic-slice_fusion
  (24 shorter events, 0.5 us)
Async XLA Ops:
  7.2 78.1 %copy-start = (s32[32]{0:T(128)S(1)}, s32[32]{0:T(128)}, u32[]{:S(2)}) copy-start(s32[32]{0:T(128)} %param.9) | copy-start | bytes 388
  7.2 186.6 %all-gather.2.cloned.1.call-start = ((), (), s32[]{:S(2)}) async-start(), calls=%async_computation | async-start | bytes 6488064 | tf_op jit(solution)/shard_map/all_gather | solution.py:15
  129.0 68.7 %copy-start.1 = (f32[256,128]{1,0:T(8,128)}, f32[256,128]{1,0:T(8,128)S(1)}, u32[]{:S(2)}) copy-start(f32[256,128]{1,0:T(8,128)S(1)} %get-tuple-element.136) | copy-start | bytes 393220
Sparse Core Ops, SparseCore 0:
  124.0 69.6 all-gather.1
